TPU v7x, 32 devices: a whole 2x2x4 slice. The times are simulated.
32 devices in a mesh: dp: 4 (over x, core), expert: 8 (over z, y).
Axes of the slice: x: 2, y: 2, z: 4, core: 2. Of those that a mesh axis runs over, the one named last changes fastest.
Arguments:
- tokens: bfloat16 [4096, 2048], P(('dp', 'expert')), may hold values from -6 to 6
- cotangent: bfloat16 [4096, 2048], P(('dp', 'expert')), may hold values from -1.5 to 1.5
- gate_score: bfloat16 [4096], P(('dp', 'expert')), may hold values from 0.19921875 to 1
- block_expert: int32 [256], P(('dp', 'expert')), may hold values from 0 to 7, as said below
- expert_slot: int32 [8], replicated, may hold values from 0 to 7, each once
- up_weight: bfloat16 [8, 2048, 704], P('expert'), may hold values from -0.125 to 0.125
- down_weight: bfloat16 [8, 2048, 704], P('expert'), may hold values from -0.21875 to 0.21875
Outputs:
- token_grad: bfloat16 [4096, 2048], P(('dp', 'expert'))
- gate_grad: bfloat16 [4096], P(('dp', 'expert'))
- grad_up: bfloat16 [8, 2048, 704], P('expert', 'dp')
- grad_down: bfloat16 [8, 2048, 704], P('expert', 'dp')
Inputs may be any that keep to these rules, and one draw needn't show every extreme that they name: `block_expert`: the 8 blocks of each device name every expert exactly once. `expert_slot`: each slot holds exactly one expert.
All inputs are finite; a program needn't handle non-finite values.
Results may differ from a plain program's by a relative error of at most 0.0085.
Values may be sent and summed in bfloat16 or wider, within the bound.
A program may use at most 64 MiB of HBM per device.

v0:
```python
import jax
import jax.numpy as jnp
from jax import lax
from jax.sharding import PartitionSpec as P


def silu_slope(pre_act):
    logistic = jax.nn.sigmoid(pre_act)
    return logistic * (1.0 + pre_act * (1.0 - logistic))


def arrange(values, order_index, peer_count):
    shaped = values.reshape((peer_count, values.shape[0] // peer_count) + values.shape[1:])
    return jnp.take(shaped, order_index, axis=0).reshape(values.shape)


def local(tokens, cotangent, gate_score, block_expert, expert_slot, up_weight, down_weight):
    row_count, model_width = tokens.shape
    hidden_width = up_weight.shape[2]
    peer_count = lax.axis_size("expert")
    share_rows = model_width // lax.axis_size("dp")
    expert_count = expert_slot.shape[0]
    chosen = (block_expert[:, None] == jnp.arange(expert_count, dtype=jnp.int32)[None, :]).astype(
        jnp.int32
    )
    block_slot = jnp.sum(chosen * expert_slot[None, :], axis=1)
    places = jnp.arange(peer_count, dtype=jnp.int32)
    matches = (block_slot[None, :] == places[:, None]).astype(jnp.int32)
    source = jnp.sum(matches * places[None, :], axis=1)
    outbound = (
        arrange(tokens, source, peer_count),
        arrange(cotangent, source, peer_count),
        arrange(gate_score, source, peer_count),
    )
    inputs, upstream, gate_rows = (
        lax.all_to_all(outbound[0], "expert", split_axis=0, concat_axis=0, tiled=True),
        lax.all_to_all(outbound[1], "expert", split_axis=0, concat_axis=0, tiled=True),
        lax.all_to_all(outbound[2], "expert", split_axis=0, concat_axis=0, tiled=True),
    )
    up_mat = up_weight[0]
    down_mat = down_weight[0]
    contract_last = (((1,), (1,)), ((), ()))
    pre_act = jnp.dot(inputs, up_mat, preferred_element_type=jnp.float32)
    hidden = jax.nn.silu(pre_act).astype(jnp.bfloat16)
    expert_out = lax.dot_general(
        hidden, down_mat, contract_last, preferred_element_type=jnp.float32
    )
    gate_grad = jnp.sum(upstream.astype(jnp.float32) * expert_out, axis=1).astype(jnp.bfloat16)
    scaled = (gate_rows.astype(jnp.float32)[:, None] * upstream.astype(jnp.float32)).astype(
        jnp.bfloat16
    )
    hidden_grad = jnp.dot(scaled, down_mat, preferred_element_type=jnp.float32)
    pre_grad = (hidden_grad * silu_slope(pre_act)).astype(jnp.bfloat16)
    input_grad = lax.dot_general(
        pre_grad, up_mat, contract_last, preferred_element_type=jnp.float32
    ).astype(jnp.bfloat16)
    returned, gate_back = (
        lax.all_to_all(input_grad, "expert", split_axis=0, concat_axis=0, tiled=True),
        lax.all_to_all(gate_grad, "expert", split_axis=0, concat_axis=0, tiled=True),
    )
    columns = (
        lax.all_to_all(inputs, "dp", split_axis=1, concat_axis=0, tiled=True),
        lax.all_to_all(scaled, "dp", split_axis=1, concat_axis=0, tiled=True),
    )
    pieces = (
        lax.all_gather(pre_grad, "dp", axis=0, tiled=True),
        lax.all_gather(hidden, "dp", axis=0, tiled=True),
    )
    row_total = pieces[0].shape[0]
    shards = row_total // row_count
    input_rows = columns[0].reshape(shards, row_count, share_rows)
    scaled_rows = columns[1].reshape(shards, row_count, share_rows)
    grad_rows = pieces[0].reshape(shards, row_count, hidden_width)
    hidden_rows = pieces[1].reshape(shards, row_count, hidden_width)
    up_partial = jnp.einsum(
        "krc,krh->kch", input_rows, grad_rows, preferred_element_type=jnp.float32
    ).astype(jnp.bfloat16)
    down_partial = jnp.einsum(
        "krc,krh->kch", scaled_rows, hidden_rows, preferred_element_type=jnp.float32
    ).astype(jnp.bfloat16)
    grad_up = jnp.sum(up_partial.astype(jnp.float32), axis=0)
    grad_down = jnp.sum(down_partial.astype(jnp.float32), axis=0)
    token_grad = arrange(returned, block_slot, peer_count)
    gate_out = arrange(gate_back, block_slot, peer_count)
    return (
        token_grad,
        gate_out,
        grad_up.astype(jnp.bfloat16)[None],
        grad_down.astype(jnp.bfloat16)[None],
    )


def solution(mesh):
    return jax.shard_map(
        local,
        mesh=mesh,
        in_specs=(
            P(("dp", "expert"), None),
            P(("dp", "expert"), None),
            P(("dp", "expert")),
            P(("dp", "expert")),
            P(),
            P("expert", None, None),
            P("expert", None, None),
        ),
        out_specs=(
            P(("dp", "expert"), None),
            P(("dp", "expert")),
            P("expert", "dp", None),
            P("expert", "dp", None),
        ),
        check_vma=False,
    )
```

profile of v0, /device:TPU:0, one launch (start us, length us, event | category | flops | bytes accessed | tf_op | source)
XLA Modules:
  0.0 127.9 jit_solution(4773708059999306015)
XLA Ops:
  0.6 1.0 select_reduce_fusion.1
  1.8 0.7 reshape.112
  3.2 0.6 copy.31
  3.8 7.3 %all-to-all-start = ((bf16[8,16,1]{1,2,0:T(2,128)(2,1)}), bf16[8,16,1]{1,2,0:T(2,128)(2,1)S(1)}, u32[]{:S(2)}, u32[]{:S(2)}) async-start(bf16[8,16,1]{1,2,0:T(2,128)(2,1)} %copy.31), calls=%async_computation | async-start | bytes 8192 | tf_op jit(solution)/shard_map/all_to_all | solution.py:38
  11.1 2.4 %gather_fusion.2 = bf16[8,16,2048]{2,1,0:T(8,128)(2,1)} fusion(bf16[8,16,2048]{2,1,0:T(8,128)(2,1)} %bitcast.67, s32[1024]{0:T(1024)S(1)} %pad_clamp_fusion.1), kind=kCustom, calls=%fused_computation.3.clone | custom fusion | bytes 1048608 | tf_op jit(solution)/shard_map/jit(_take)/gather | solution.py:14
  13.5 2.4 %gather_fusion.1 = bf16[8,16,2048]{2,1,0:T(8,128)(2,1)} fusion(bf16[8,16,2048]{2,1,0:T(8,128)(2,1)} %bitcast.68, s32[1024]{0:T(1024)S(1)} %pad_clamp_fusion.1), kind=kCustom, calls=%fused_computation.1.clone | custom fusion | bytes 1048608 | tf_op jit(solution)/shard_map/jit(_take)/gather | solution.py:14
  15.9 2.2 %broadcast_select_fusion.1 = (bf16[8,16,2048]{2,1,0:T(8,128)(2,1)S(1)}, bf16[8,16,2048]{2,1,0:T(8,128)(2,1)}) fusion(bf16[8,16,2048]{2,1,0:T(8,128)(2,1)} %gather_fusion.2, pred[8]{0:T(512)(128)(4,1)S(1)} %compare_and_fusion.1, bf16[8,16,2048]{2,1,0:T(8,128)(2,1)} %gather_fusion.1), kind=kLoop, calls=%fused_computation.30 | loop fusion | flops 524288 | bytes 2097160 | tf_op jit(solution)/shard_map/jit(_take)/select_n | solution.py:14
  18.0 19.8 %all_to_all.68 = bf16[8,16,2048]{2,1,0:T(8,128)(2,1)} all-to-all(bf16[8,16,2048]{2,1,0:T(8,128)(2,1)S(1)} %get-tuple-element.8), channel_id=1, replica_groups=mesh['dp'=4,'expert'=8] {'expert'}, dimensions={0} | all-to-all | bytes 1048576 | tf_op jit(solution)/shard_map/all_to_all | solution.py:36
  37.9 3.6 %all-to-all-start.1 = ((bf16[8,16,2048]{2,1,0:T(8,128)(2,1)}), bf16[8,16,2048]{2,1,0:T(8,128)(2,1)S(1)}, u32[]{:S(2)}, u32[]{:S(2)}) async-start(bf16[8,16,2048]{2,1,0:T(8,128)(2,1)} %get-tuple-element.9), calls=%async_computation.1 | async-start | bytes 1048576 | tf_op jit(solution)/shard_map/all_to_all | solution.py:37
  41.6 2.8 %multiply_convert_fusion.1 = (bf16[128,704]{0,1:T(8,128)(2,1)}, f32[128,704]{0,1:T(8,128)}) fusion(bf16[128,2048]{1,0:T(8,128)(2,1)} %bitcast.65, bf16[1,2048,704]{1,2,0:T(8,128)(2,1)S(1)} %copy-done), kind=kOutput, calls=%fused_computation.32 | convolution fusion | flops 369549312 | bytes 3948544 | tf_op jit(solution)/shard_map/dot_general | solution.py:43
  44.4 11.1 %all-to-all-done.1 = bf16[8,16,2048]{2,1,0:T(8,128)(2,1)S(1)} async-done(((bf16[8,16,2048]{2,1,0:T(8,128)(2,1)}), bf16[8,16,2048]{2,1,0:T(8,128)(2,1)S(1)}, u32[]{:S(2)}, u32[]{:S(2)}) %all-to-all-start.1) | async-done | bytes 524320 | tf_op jit(solution)/shard_map/all_to_all | solution.py:37
  55.6 2.6 %fusion.14 = bf16[128]{0:T(256)(128)(2,1)S(1)} fusion(f32[128,2048]{1,0:T(8,128)S(1)} %bitcast.64, bf16[128,704]{0,1:T(8,128)(2,1)} %get-tuple-element.10, bf16[1,2048,704]{1,2,0:T(8,128)(2,1)} %param.17), kind=kOutput, calls=%fused_computation.17 | convolution fusion | flops 369622912 | bytes 4112640 | tf_op jit(solution)/shard_map/dot_general | solution.py:45
  58.3 0.7 convert_element_type.98
  58.9 3.6 %all-to-all-start.4 = ((bf16[8,16,1]{1,2,0:T(2,128)(2,1)}), bf16[8,16,1]{1,2,0:T(2,128)(2,1)S(1)}, u32[]{:S(2)}, u32[]{:S(2)}) async-start(bf16[8,16,1]{1,2,0:T(2,128)(2,1)} %convert_element_type.98), calls=%async_computation.4 | async-start | bytes 8192 | tf_op jit(solution)/shard_map/all_to_all | solution.py:59
  62.6 0.9 multiply_convert_fusion
  63.5 2.2 %all_to_all.56 = bf16[128,4,512]{2,1,0:T(4,128)(2,1)} reshape(bf16[8,16,2048]{2,1,0:T(8,128)(2,1)} %all_to_all.68) | data formatting | bytes 1048576 | tf_op jit(solution)/shard_map/all_to_all | solution.py:62
  65.8 1.9 %copy.34 = bf16[128,4,512]{2,0,1:T(8,128)(2,1)} copy(bf16[128,4,512]{2,1,0:T(4,128)(2,1)} %all_to_all.56) | data formatting | bytes 1048576 | tf_op jit(solution)/shard_map/all_to_all | solution.py:62
  67.7 1.7 %reshape.123 = f32[128,4,512]{2,1,0:T(4,128)} reshape(bf16[8,16,2048]{2,1,0:T(8,128)(2,1)S(1)} %all-to-all-done.1) | data formatting | bytes 1572864 | tf_op jit(solution)/shard_map/convert_element_type | solution.py:49
  69.4 4.1 %all-to-all-start.5 = ((bf16[128,4,512]{2,0,1:T(8,128)(2,1)}), bf16[128,4,512]{2,0,1:T(8,128)(2,1)}, u32[]{:S(2)}, u32[]{:S(2)}) async-start(bf16[128,4,512]{2,0,1:T(8,128)(2,1)} %copy.34), calls=%async_computation.5 | async-start | bytes 1048576 | tf_op jit(solution)/shard_map/all_to_all | solution.py:62
  73.6 2.3 %fusion.23 = bf16[128,4,512]{2,0,1:T(8,128)(2,1)} fusion(f32[128,4,512]{2,1,0:T(4,128)} %reshape.123, f32[128]{0:T(128)S(1)} %reshape.122), kind=kLoop, calls=%fused_computation.21 | loop fusion | flops 524288 | bytes 1573376 | tf_op jit(solution)/shard_map/convert_element_type | solution.py:49
  75.9 2.9 %fusion.20 = bf16[128,704]{0,1:T(8,128)(2,1)S(1)} fusion(bf16[128,2048]{1,0:T(8,128)(2,1)} %bitcast.66, bf16[1,2048,704]{1,2,0:T(8,128)(2,1)} %param.17, f32[128,704]{0,1:T(8,128)} %get-tuple-element.11), kind=kOutput, calls=%fused_computation.19 | convolution fusion | flops 369909760 | bytes 3948544 | tf_op jit(solution)/shard_map/dot_general | solution.py:52
  78.8 3.6 %all-to-all-done.5 = bf16[128,4,512]{2,0,1:T(8,128)(2,1)} async-done(((bf16[128,4,512]{2,0,1:T(8,128)(2,1)}), bf16[128,4,512]{2,0,1:T(8,128)(2,1)}, u32[]{:S(2)}, u32[]{:S(2)}) %all-to-all-start.5) | async-done | bytes 524320 | tf_op jit(solution)/shard_map/all_to_all | solution.py:62
  82.5 4.1 %all-to-all-start.6 = ((bf16[128,4,512]{2,0,1:T(8,128)(2,1)}), bf16[128,4,512]{2,0,1:T(8,128)(2,1)}, u32[]{:S(2)}, u32[]{:S(2)}) async-start(bf16[128,4,512]{2,0,1:T(8,128)(2,1)} %fusion.23), calls=%async_computation.6 | async-start | bytes 1048576 | tf_op jit(solution)/shard_map/all_to_all | solution.py:63
  86.6 14.0 %all_gather.6 = bf16[512,704]{0,1:T(8,128)(2,1)} all-gather(bf16[128,704]{0,1:T(8,128)(2,1)S(1)} %fusion.20), channel_id=1, replica_groups=mesh['dp'=4,'expert'=8] {'dp'}, dimensions={0}, use_global_device_ids=true | all-gather | bytes 901120 | tf_op jit(solution)/shard_map/all_gather | solution.py:66
  100.6 1.4 %fusion.11 = bf16[128,2048]{1,0:T(8,128)(2,1)} fusion(bf16[128,704]{0,1:T(8,128)(2,1)S(1)} %fusion.20, bf16[1,2048,704]{1,2,0:T(8,128)(2,1)S(1)} %copy-done), kind=kOutput, calls=%fused_computation.16 | convolution fusion | flops 369360896 | bytes 3588096 | tf_op jit(solution)/shard_map/dot_general | solution.py:54
  102.0 6.0 %all-to-all-start.3 = ((bf16[8,16,2048]{2,1,0:T(8,128)(2,1)}), bf16[8,16,2048]{2,1,0:T(8,128)(2,1)S(1)}, u32[]{:S(2)}, u32[]{:S(2)}) async-start(bf16[8,16,2048]{2,1,0:T(8,128)(2,1)} %bitcast.8), calls=%async_computation.3 | async-start | bytes 1048576 | tf_op jit(solution)/shard_map/all_to_all | solution.py:58
  108.0 8.9 %all_gather.7 = bf16[512,704]{0,1:T(8,128)(2,1)} all-gather(bf16[128,704]{0,1:T(8,128)(2,1)} %get-tuple-element.10), channel_id=1, replica_groups=mesh['dp'=4,'expert'=8] {'dp'}, dimensions={0}, use_global_device_ids=true | all-gather | bytes 901120 | tf_op jit(solution)/shard_map/all_gather | solution.py:67
  117.6 0.6 reshape.117
  118.2 3.2 %convert_reduce_fusion.1 = bf16[512,704]{0,1:T(8,128)(2,1)} fusion(bf16[128,4,512]{2,0,1:T(8,128)(2,1)} %all-to-all-done.5, bf16[512,704]{0,1:T(8,128)(2,1)} %all_gather.6), kind=kOutput, calls=%fused_computation.14 | convolution fusion | flops 371621888 | bytes 1966080 | tf_op jit(solution)/shard_map/krc,krh->kch/dot_general | solution.py:75
  121.4 3.2 %convert_reduce_fusion = bf16[512,704]{0,1:T(8,128)(2,1)} fusion(bf16[128,4,512]{2,0,1:T(8,128)(2,1)} %all-to-all-done.6, bf16[512,704]{0,1:T(8,128)(2,1)} %all_gather.7), kind=kOutput, calls=%fused_computation.13 | convolution fusion | flops 371621888 | bytes 1966080 | tf_op jit(solution)/shard_map/krc,krh->kch/dot_general | solution.py:78
  124.5 1.4 %gather_fusion.3 = bf16[8,16,2048]{2,1,0:T(8,128)(2,1)} fusion(bf16[8,16,2048]{2,1,0:T(8,128)(2,1)S(1)} %all-to-all-done.3, s32[1024]{0:T(1024)S(1)} %pad_clamp_fusion), kind=kCustom, calls=%fused_computation.4.clone | custom fusion | bytes 1048608 | tf_op jit(solution)/shard_map/jit(_take)/gather | solution.py:14
  125.9 1.9 %broadcast_select_fusion = bf16[8,16,2048]{2,1,0:T(8,128)(2,1)} fusion(bf16[8,16,2048]{2,1,0:T(8,128)(2,1)} %gather_fusion.3, pred[8]{0:T(512)(128)(4,1)S(1)} %compare_and_fusion), kind=kLoop, calls=%fused_computation.29 | loop fusion | flops 262144 | bytes 1048584 | tf_op jit(solution)/shard_map/jit(_take)/select_n | solution.py:14
  (21 shorter events, 1.6 us)
Async XLA Ops:
  0.6 41.0 %copy-start = (bf16[1,2048,704]{1,2,0:T(8,128)(2,1)S(1)}, bf16[1,2048,704]{1,2,0:T(8,128)(2,1)}, u32[]{:S(2)}) copy-start(bf16[1,2048,704]{1,2,0:T(8,128)(2,1)} %param.16) | copy-start | bytes 8650756
  3.8 14.3 %all-to-all-start = ((bf16[8,16,1]{1,2,0:T(2,128)(2,1)}), bf16[8,16,1]{1,2,0:T(2,128)(2,1)S(1)}, u32[]{:S(2)}, u32[]{:S(2)}) async-start(bf16[8,16,1]{1,2,0:T(2,128)(2,1)} %copy.31), calls=%async_computation | async-start | bytes 8192 | tf_op jit(solution)/shard_map/all_to_all | solution.py:38
  37.9 17.7 %all-to-all-start.1 = ((bf16[8,16,2048]{2,1,0:T(8,128)(2,1)}), bf16[8,16,2048]{2,1,0:T(8,128)(2,1)S(1)}, u32[]{:S(2)}, u32[]{:S(2)}) async-start(bf16[8,16,2048]{2,1,0:T(8,128)(2,1)} %get-tuple-element.9), calls=%async_computation.1 | async-start | bytes 1048576 | tf_op jit(solution)/shard_map/all_to_all | solution.py:37
  58.9 10.5 %all-to-all-start.4 = ((bf16[8,16,1]{1,2,0:T(2,128)(2,1)}), bf16[8,16,1]{1,2,0:T(2,128)(2,1)S(1)}, u32[]{:S(2)}, u32[]{:S(2)}) async-start(bf16[8,16,1]{1,2,0:T(2,128)(2,1)} %convert_element_type.98), calls=%async_computation.4 | async-start | bytes 8192 | tf_op jit(solution)/shard_map/all_to_all | solution.py:59
  69.4 13.1 %all-to-all-start.5 = ((bf16[128,4,512]{2,0,1:T(8,128)(2,1)}), bf16[128,4,512]{2,0,1:T(8,128)(2,1)}, u32[]{:S(2)}, u32[]{:S(2)}) async-start(bf16[128,4,512]{2,0,1:T(8,128)(2,1)} %copy.34), calls=%async_computation.5 | async-start | bytes 1048576 | tf_op jit(solution)/shard_map/all_to_all | solution.py:62
  82.5 19.5 %all-to-all-start.6 = ((bf16[128,4,512]{2,0,1:T(8,128)(2,1)}), bf16[128,4,512]{2,0,1:T(8,128)(2,1)}, u32[]{:S(2)}, u32[]{:S(2)}) async-start(bf16[128,4,512]{2,0,1:T(8,128)(2,1)} %fusion.23), calls=%async_computation.6 | async-start | bytes 1048576 | tf_op jit(solution)/shard_map/all_to_all | solution.py:63
  102.0 22.5 %all-to-all-start.3 = ((bf16[8,16,2048]{2,1,0:T(8,128)(2,1)}), bf16[8,16,2048]{2,1,0:T(8,128)(2,1)S(1)}, u32[]{:S(2)}, u32[]{:S(2)}) async-start(bf16[8,16,2048]{2,1,0:T(8,128)(2,1)} %bitcast.8), calls=%async_computation.3 | async-start | bytes 1048576 | tf_op jit(solution)/shard_map/all_to_all | solution.py:58
where the time goes:
time: 129 us; the launch traced here: 128 us
  blocking collectives  42.8 us (33%)
  starting transfers between devices  28.8 us (22%)
  matrix products  16 us (12%)
  local copies, waits for them, and re-layouts  15.9 us (12%)
  waiting for transfers between devices  14.8 us (11%)
  other arithmetic  8.8 us (7%)
    all_to_all x1, blocking collectives, local(): lax.all_to_all(outbound[0], 'expert', split_axis=0, concat_axis=0, tiled=...  19.8 us
    all_gather x1, blocking collectives, local(): lax.all_gather(pre_grad, 'dp', axis=0, tiled=True)  14 us
    all_to_all x1, waiting for transfers between devices, local(): lax.all_to_all(outbound[1], 'expert', split_axis=0, concat_axis=0, tiled=...  11.1 us
    all_gather x1, blocking collectives, local(): lax.all_gather(hidden, 'dp', axis=0, tiled=True)  8.95 us
    gather x5, local copies, waits for them, and re-layouts, arrange(): return jnp.take(shaped, order_index, axis=0).reshape(values.shape)  7.33 us
    all_to_all x1, starting transfers between devices, local(): lax.all_to_all(outbound[2], 'expert', split_axis=0, concat_axis=0, tiled=...  7.28 us
    all_to_all x1, starting transfers between devices, local(): lax.all_to_all(input_grad, 'expert', split_axis=0, concat_axis=0, tiled=T...  6 us
    select_n x5, other arithmetic, arrange(): return jnp.take(shaped, order_index, axis=0).reshape(values.shape)  4.18 us
  transfers between devices with their start and end apart: 6, of which 2 were waited for; matrix products, arithmetic and copies ran while one was open for 22% of the time, Pallas kernels for 0%

commit v1 on v0

--- a/solution.py
+++ b/solution.py
@@ -2,6 +2,29 @@
 import jax.numpy as jnp
 from jax import lax
 from jax.sharding import PartitionSpec as P
+
+
+def in_blocks(shard, dim, size):
+    dims = shard.shape
+    blocks = shard.reshape(*dims[:dim], size, dims[dim] // size, *dims[dim + 1 :])
+    return jnp.moveaxis(blocks, dim, 0)
+
+
+def laid_out(blocks, dim):
+    blocks = jnp.moveaxis(blocks, 0, dim)
+    lengths = blocks.shape
+    return blocks.reshape(*lengths[:dim], lengths[dim] * lengths[dim + 1], *lengths[dim + 2 :])
+
+
+def swapped_with_each(shard, axis, split_dim, concat_dim):
+    size, index = (lax.axis_size(axis), lax.axis_index(axis))
+    parts = in_blocks(shard, split_dim, size)
+    done = [parts[index]]
+    for step in range(1, size):
+        sent = parts[index ^ step]
+        done.append(lax.ppermute(sent, axis, [(i, i ^ step) for i in range(size)]))
+    parts = jnp.stack(done)[index ^ jnp.arange(size)]
+    return laid_out(parts, concat_dim)
 
 
 def silu_slope(pre_act):
@@ -55,7 +78,7 @@
         pre_grad, up_mat, contract_last, preferred_element_type=jnp.float32
     ).astype(jnp.bfloat16)
     returned, gate_back = (
-        lax.all_to_all(input_grad, "expert", split_axis=0, concat_axis=0, tiled=True),
+        swapped_with_each(input_grad, "expert", 0, 0),
         lax.all_to_all(gate_grad, "expert", split_axis=0, concat_axis=0, tiled=True),
     )
     columns = (

time: 129 us -> 136 us (1.054)
  blocking collectives: 42.8 us -> 16.6 us
  waiting for transfers between devices: 14.8 us -> 29.8 us
  starting transfers between devices: 28.8 us -> 40.8 us
  local copies, waits for them, and re-layouts: 15.9 us -> 26.7 us
  matrix products: 16 us -> 13.2 us
  other arithmetic: 8.8 us -> 7.01 us
    all_to_all x1 -> x0, blocking collectives: 19.8 us -> none  [local(): lax.all_to_all(outbound[0], 'expert', split_axis=0, concat_axis=0, tiled=...]
    all_to_all x1, waiting for transfers between devices: 0.01 us -> 14 us  [local(): lax.all_to_all(outbound[0], 'expert', split_axis=0, concat_axis=0, tiled=...]
    ppermute x0 -> x7, starting transfers between devices: none -> 12.5 us  [swapped_with_each(): done.append(lax.ppermute(sent, axis, [(i, i ^ step) for i in range(size)]))]
    unnamed x3 -> x15, local copies, waits for them, and re-layouts: 0.01 us -> 8.81 us
    all_gather x1, blocking collectives: 14 us -> 8.82 us  [local(): lax.all_gather(pre_grad, 'dp', axis=0, tiled=True)]
    all_to_all x1, waiting for transfers between devices: 0.01 us -> 4.83 us  [local(): lax.all_to_all(scaled, 'dp', split_axis=1, concat_axis=0, tiled=True)]
    all_to_all x1, waiting for transfers between devices: 3.64 us -> 0.01 us  [local(): lax.all_to_all(inputs, 'dp', split_axis=1, concat_axis=0, tiled=True)]
    gather x0 -> x1, local copies, waits for them, and re-layouts: none -> 2.41 us  [swapped_with_each(): parts = jnp.stack(done)[index ^ jnp.arange(size)]]
  transfers between devices with their start and end apart: 6 -> 13, of which waited for: 2 -> 5; matrix products, arithmetic and copies ran while one was open for 22% -> 25% of each run, Pallas kernels for 0% -> 0%
where the time goes in v1:
time: 136 us; the launch traced here: 135 us
  starting transfers between devices  40.8 us (30%)
  waiting for transfers between devices  29.8 us (22%)
  local copies, waits for them, and re-layouts  26.7 us (20%)
  blocking collectives  16.6 us (12%)
  matrix products  13.2 us (10%)
  other arithmetic  7.01 us (5%)
    all_to_all x1, waiting for transfers between devices, local(): lax.all_to_all(outbound[0], 'expert', split_axis=0, concat_axis=0, tiled=...  14 us
    ppermute x7, starting transfers between devices, swapped_with_each(): done.append(lax.ppermute(sent, axis, [(i, i ^ step) for i in range(size)]))  12.5 us
    all_to_all x1, waiting for transfers between devices, local(): lax.all_to_all(outbound[1], 'expert', split_axis=0, concat_axis=0, tiled=...  10.8 us
    all_gather x1, blocking collectives, local(): lax.all_gather(pre_grad, 'dp', axis=0, tiled=True)  8.82 us
    unnamed x15, local copies, waits for them, and re-layouts  8.81 us
    all_gather x1, blocking collectives, local(): lax.all_gather(hidden, 'dp', axis=0, tiled=True)  7.8 us
    all_to_all x1, starting transfers between devices, local(): lax.all_to_all(outbound[2], 'expert', split_axis=0, concat_axis=0, tiled=...  7.28 us
    gather x5, local copies, waits for them, and re-layouts, arrange(): return jnp.take(shaped, order_index, axis=0).reshape(values.shape)  6.79 us
  transfers between devices with their start and end apart: 13, of which 5 were waited for; matrix products, arithmetic and copies ran while one was open for 25% of the time, Pallas kernels for 0%

profile of v1, /device:TPU:0, one launch (start us, length us, event | category | flops | bytes accessed | tf_op | source)
XLA Modules:
  0.0 134.9 jit_solution(15091418735628732627)
XLA Ops:
  3.8 7.3 %all-to-all-start = ((bf16[8,16,1]{1,2,0:T(2,128)(2,1)}), bf16[8,16,1]{1,2,0:T(2,128)(2,1)S(1)}, u32[]{:S(2)}, u32[]{:S(2)}) async-start(bf16[8,16,1]{1,2,0:T(2,128)(2,1)} %copy.31), calls=%async_computation | async-start | bytes 8192 | tf_op jit(solution)/shard_map/all_to_all | solution.py:61
  11.1 1.6 %gather_fusion.3 = bf16[8,16,2048]{2,1,0:T(8,128)(2,1)S(1)} fusion(bf16[8,16,2048]{2,1,0:T(8,128)(2,1)} %bitcast.98, s32[1024]{0:T(1024)S(1)} %pad_clamp_fusion.2), kind=kCustom, calls=%fused_computation.3.clone | custom fusion | bytes 1048608 | tf_op jit(solution)/shard_map/jit(_take)/gather | solution.py:37
  12.7 2.4 %gather_fusion.2 = bf16[8,16,2048]{2,1,0:T(8,128)(2,1)} fusion(bf16[8,16,2048]{2,1,0:T(8,128)(2,1)} %bitcast.99, s32[1024]{0:T(1024)S(1)} %pad_clamp_fusion.2), kind=kCustom, calls=%fused_computation.1.clone | custom fusion | bytes 1048608 | tf_op jit(solution)/shard_map/jit(_take)/gather | solution.py:37
  15.1 2.2 %broadcast_select_fusion.1 = (bf16[8,16,2048]{2,1,0:T(8,128)(2,1)}, bf16[8,16,2048]{2,1,0:T(8,128)(2,1)}) fusion(bf16[8,16,2048]{2,1,0:T(8,128)(2,1)S(1)} %gather_fusion.3, pred[8]{0:T(512)(128)(4,1)S(1)} %compare_and_fusion.1, bf16[8,16,2048]{2,1,0:T(8,128)(2,1)} %gather_fusion.2), kind=kLoop, calls=%fused_computation.31 | loop fusion | flops 524288 | bytes 2097160 | tf_op jit(solution)/shard_map/jit(_take)/select_n | solution.py:37
  17.5 5.8 %all-to-all-start.2 = ((bf16[8,16,2048]{2,1,0:T(8,128)(2,1)}), bf16[8,16,2048]{2,1,0:T(8,128)(2,1)S(1)}, u32[]{:S(2)}, u32[]{:S(2)}) async-start(bf16[8,16,2048]{2,1,0:T(8,128)(2,1)} %get-tuple-element.16), calls=%async_computation.2 | async-start | bytes 1048576 | tf_op jit(solution)/shard_map/all_to_all | solution.py:59
  23.3 14.0 %all-to-all-done.2 = bf16[8,16,2048]{2,1,0:T(8,128)(2,1)S(1)} async-done(((bf16[8,16,2048]{2,1,0:T(8,128)(2,1)}), bf16[8,16,2048]{2,1,0:T(8,128)(2,1)S(1)}, u32[]{:S(2)}, u32[]{:S(2)}) %all-to-all-start.2) | async-done | bytes 524320 | tf_op jit(solution)/shard_map/all_to_all | solution.py:59
  38.0 3.6 %all-to-all-start.1 = ((bf16[8,16,2048]{2,1,0:T(8,128)(2,1)}), bf16[8,16,2048]{2,1,0:T(8,128)(2,1)S(1)}, u32[]{:S(2)}, u32[]{:S(2)}) async-start(bf16[8,16,2048]{2,1,0:T(8,128)(2,1)} %get-tuple-element.17), calls=%async_computation.1 | async-start | bytes 1048576 | tf_op jit(solution)/shard_map/all_to_all | solution.py:60
  42.4 2.8 %multiply_convert_fusion.1 = (bf16[128,704]{0,1:T(8,128)(2,1)}, f32[128,704]{0,1:T(8,128)}) fusion(bf16[128,2048]{1,0:T(8,128)(2,1)} %bitcast.96, bf16[1,2048,704]{1,2,0:T(8,128)(2,1)S(1)} %copy-done), kind=kOutput, calls=%fused_computation.33 | convolution fusion | flops 369549312 | bytes 3948544 | tf_op jit(solution)/shard_map/dot_general | solution.py:66
  45.1 10.8 %all-to-all-done.1 = bf16[8,16,2048]{2,1,0:T(8,128)(2,1)S(1)} async-done(((bf16[8,16,2048]{2,1,0:T(8,128)(2,1)}), bf16[8,16,2048]{2,1,0:T(8,128)(2,1)S(1)}, u32[]{:S(2)}, u32[]{:S(2)}) %all-to-all-start.1) | async-done | bytes 524320 | tf_op jit(solution)/shard_map/all_to_all | solution.py:60
  56.1 2.8 %fusion.20 = bf16[128,704]{0,1:T(8,128)(2,1)S(1)} fusion(bf16[128,2048]{1,0:T(8,128)(2,1)S(1)} %bitcast.97, bf16[1,2048,704]{1,2,0:T(8,128)(2,1)} %param.17, f32[128,704]{0,1:T(8,128)} %get-tuple-element.19), kind=kOutput, calls=%fused_computation.20 | convolution fusion | flops 369909760 | bytes 3948544 | tf_op jit(solution)/shard_map/dot_general | solution.py:75
  59.5 8.8 %all_gather.6 = bf16[512,704]{0,1:T(8,128)(2,1)} all-gather(bf16[128,704]{0,1:T(8,128)(2,1)S(1)} %fusion.20), channel_id=1, replica_groups=mesh['dp'=4,'expert'=8] {'dp'}, dimensions={0}, use_global_device_ids=true | all-gather | bytes 901120 | tf_op jit(solution)/shard_map/all_gather | solution.py:89
  70.5 2.1 %collective-permute-start.2 = (bf16[16,2048]{1,0:T(8,128)(2,1)}, bf16[16,2048]{1,0:T(8,128)(2,1)}, u32[]{:S(2)}, u32[]{:S(2)}) collective-permute-start(bf16[16,2048]{1,0:T(8,128)(2,1)} %get-tuple-element.10), channel_id=1, source_target_pairs={{0,3},{1,2},{2,1},{3,0},{4,7},{5,6},{6,5},{7,4},{8,11},{9,10},{10,... | collective-permute-start | bytes 196616 | tf_op jit(solution)/shard_map/ppermute | solution.py:25
  72.9 3.4 %collective-permute-start.4 = (bf16[16,2048]{1,0:T(8,128)(2,1)}, bf16[16,2048]{1,0:T(8,128)(2,1)}, u32[]{:S(2)}, u32[]{:S(2)}) collective-permute-start(bf16[16,2048]{1,0:T(8,128)(2,1)} %get-tuple-element.8), channel_id=1, source_target_pairs={{0,5},{1,4},{2,7},{3,6},{4,1},{5,0},{6,3},{7,2},{8,13},{9,12},{10,... | collective-permute-start | bytes 196616 | tf_op jit(solution)/shard_map/ppermute | solution.py:25
  76.3 7.8 %all_gather.7 = bf16[512,704]{0,1:T(8,128)(2,1)} all-gather(bf16[128,704]{0,1:T(8,128)(2,1)S(1)} %copy-done.3), channel_id=1, replica_groups=mesh['dp'=4,'expert'=8] {'dp'}, dimensions={0}, use_global_device_ids=true | all-gather | bytes 901120 | tf_op jit(solution)/shard_map/all_gather | solution.py:90
  85.6 3.3 %all-to-all-start.3 = ((bf16[8,16,1]{1,2,0:T(2,128)(2,1)}), bf16[8,16,1]{1,2,0:T(2,128)(2,1)S(1)}, u32[]{:S(2)}, u32[]{:S(2)}) async-start(bf16[8,16,1]{1,2,0:T(2,128)(2,1)} %convert_element_type.98), calls=%async_computation.3 | async-start | bytes 8192 | tf_op jit(solution)/shard_map/all_to_all | solution.py:82
  88.9 1.7 %reshape.139 = f32[128,4,512]{2,1,0:T(4,128)} reshape(bf16[8,16,2048]{2,1,0:T(8,128)(2,1)S(1)} %all-to-all-done.1) | data formatting | bytes 1572864 | tf_op jit(solution)/shard_map/convert_element_type | solution.py:72
  90.6 2.4 %fusion.23 = bf16[128,4,512]{2,0,1:T(8,128)(2,1)} fusion(f32[128,4,512]{2,1,0:T(4,128)} %reshape.139, f32[128]{0:T(128)} %reshape.138), kind=kLoop, calls=%fused_computation.22 | loop fusion | flops 524288 | bytes 1573376 | tf_op jit(solution)/shard_map/convert_element_type | solution.py:72
  93.0 1.4 %all_to_all.48 = bf16[128,4,512]{2,1,0:T(4,128)(2,1)S(1)} reshape(bf16[8,16,2048]{2,1,0:T(8,128)(2,1)} %copy-done.2) | data formatting | bytes 1048576 | tf_op jit(solution)/shard_map/all_to_all | solution.py:85
  95.3 4.1 %all-to-all-start.4 = ((bf16[128,4,512]{2,0,1:T(8,128)(2,1)}), bf16[128,4,512]{2,0,1:T(8,128)(2,1)}, u32[]{:S(2)}, u32[]{:S(2)}) async-start(bf16[128,4,512]{2,0,1:T(8,128)(2,1)} %copy.34), calls=%async_computation.4 | async-start | bytes 1048576 | tf_op jit(solution)/shard_map/all_to_all | solution.py:85
  100.7 3.8 %collective-permute-start.5 = (bf16[16,2048]{1,0:T(8,128)(2,1)S(1)}, bf16[16,2048]{1,0:T(8,128)(2,1)S(1)}, u32[]{:S(2)}, u32[]{:S(2)}) collective-permute-start(bf16[16,2048]{1,0:T(8,128)(2,1)S(1)} %get-tuple-element.7), channel_id=1, source_target_pairs={{0,6},{1,7},{2,4},{3,5},{4,2},{5,3},{6,0},{7,1},{8,14},{9,15},{10,... | collective-permute-start | bytes 196616 | tf_op jit(solution)/shard_map/ppermute | solution.py:25
  104.5 1.5 %bitcast_dynamic-update-slice_fusion.6 = bf16[8,16,2048]{2,1,0:T(8,128)(2,1)} fusion(bf16[8,16,2048]{2,1,0:T(8,128)(2,1)} %get-tuple-element.13, bf16[16,2048]{1,0:T(8,128)(2,1)} %collective-permute-done), kind=kLoop, calls=%fused_computation.41 | loop fusion | bytes 131072
  106.0 1.5 %collective-permute-start.6 = (bf16[16,2048]{1,0:T(8,128)(2,1)S(1)}, bf16[16,2048]{1,0:T(8,128)(2,1)S(1)}, u32[]{:S(2)}, u32[]{:S(2)}) collective-permute-start(bf16[16,2048]{1,0:T(8,128)(2,1)S(1)} %get-tuple-element.6), channel_id=1, source_target_pairs={{0,7},{1,6},{2,5},{3,4},{4,3},{5,2},{6,1},{7,0},{8,15},{9,14},{10,... | collective-permute-start | bytes 196616 | tf_op jit(solution)/shard_map/ppermute | solution.py:25
  107.5 1.5 %bitcast_dynamic-update-slice_fusion.5 = bf16[8,16,2048]{2,1,0:T(8,128)(2,1)} fusion(bf16[8,16,2048]{2,1,0:T(8,128)(2,1)} %bitcast_dynamic-update-slice_fusion.6, bf16[16,2048]{1,0:T(8,128)(2,1)} %collective-permute-done.1), kind=kLoop, calls=%fused_computation.40 | loop fusion | bytes 131072
  108.9 1.5 %bitcast_dynamic-update-slice_fusion.4 = bf16[8,16,2048]{2,1,0:T(8,128)(2,1)} fusion(bf16[8,16,2048]{2,1,0:T(8,128)(2,1)} %bitcast_dynamic-update-slice_fusion.5, bf16[16,2048]{1,0:T(8,128)(2,1)} %collective-permute-done.2), kind=kLoop, calls=%fused_computation.39 | loop fusion | bytes 131072
  110.4 1.5 %bitcast_dynamic-update-slice_fusion.3 = bf16[8,16,2048]{2,1,0:T(8,128)(2,1)} fusion(bf16[8,16,2048]{2,1,0:T(8,128)(2,1)} %bitcast_dynamic-update-slice_fusion.4, bf16[16,2048]{1,0:T(8,128)(2,1)} %collective-permute-done.3), kind=kLoop, calls=%fused_computation.38 | loop fusion | bytes 131072
  111.9 1.5 %bitcast_dynamic-update-slice_fusion.2 = bf16[8,16,2048]{2,1,0:T(8,128)(2,1)} fusion(bf16[8,16,2048]{2,1,0:T(8,128)(2,1)} %bitcast_dynamic-update-slice_fusion.3, bf16[16,2048]{1,0:T(8,128)(2,1)} %collective-permute-done.4), kind=kLoop, calls=%fused_computation.37 | loop fusion | bytes 131072
  114.6 2.4 %gather_fusion = bf16[8,16,2048]{2,1,0:T(8,128)(2,1)} fusion(bf16[8,16,2048]{2,1,0:T(8,128)(2,1)} %bitcast_dynamic-update-slice_fusion, s32[1024]{0:T(1024)S(1)} %pad_clamp_fusion.1), kind=kCustom, calls=%fused_computation.5 | custom fusion | bytes 1048608 | tf_op jit(solution)/shard_map/gather | solution.py:26
  117.0 1.6 %gather_fusion.4 = bf16[8,16,2048]{2,1,0:T(8,128)(2,1)S(1)} fusion(bf16[8,16,2048]{2,1,0:T(8,128)(2,1)} %gather_fusion, s32[1024]{0:T(1024)S(1)} %pad_clamp_fusion), kind=kCustom, calls=%fused_computation.4.clone | custom fusion | bytes 1048608 | tf_op jit(solution)/shard_map/jit(_take)/gather | solution.py:37
  118.7 4.2 %all-to-all-start.5 = ((bf16[128,4,512]{2,0,1:T(8,128)(2,1)}), bf16[128,4,512]{2,0,1:T(8,128)(2,1)}, u32[]{:S(2)}, u32[]{:S(2)}) async-start(bf16[128,4,512]{2,0,1:T(8,128)(2,1)} %fusion.23), calls=%async_computation.5 | async-start | bytes 1048576 | tf_op jit(solution)/shard_map/all_to_all | solution.py:86
  123.7 3.2 %convert_reduce_fusion.1 = bf16[512,704]{0,1:T(8,128)(2,1)} fusion(bf16[128,4,512]{2,0,1:T(8,128)(2,1)} %all-to-all-done.4, bf16[512,704]{0,1:T(8,128)(2,1)} %all_gather.6), kind=kOutput, calls=%fused_computation.15 | convolution fusion | flops 371621888 | bytes 1966080 | tf_op jit(solution)/shard_map/krc,krh->kch/dot_general | solution.py:98
  126.9 4.8 %all-to-all-done.5 = bf16[128,4,512]{2,0,1:T(8,128)(2,1)} async-done(((bf16[128,4,512]{2,0,1:T(8,128)(2,1)}), bf16[128,4,512]{2,0,1:T(8,128)(2,1)}, u32[]{:S(2)}, u32[]{:S(2)}) %all-to-all-start.5) | async-done | bytes 524320 | tf_op jit(solution)/shard_map/all_to_all | solution.py:86
  131.7 3.2 %convert_reduce_fusion = bf16[512,704]{0,1:T(8,128)(2,1)} fusion(bf16[128,4,512]{2,0,1:T(8,128)(2,1)} %all-to-all-done.5, bf16[512,704]{0,1:T(8,128)(2,1)} %all_gather.7), kind=kOutput, calls=%fused_computation.14 | convolution fusion | flops 371621888 | bytes 1966080 | tf_op jit(solution)/shard_map/krc,krh->kch/dot_general | solution.py:101
  (51 shorter events, 13.9 us)
Async XLA Ops:
  0.6 41.7 %copy-start = (bf16[1,2048,704]{1,2,0:T(8,128)(2,1)S(1)}, bf16[1,2048,704]{1,2,0:T(8,128)(2,1)}, u32[]{:S(2)}) copy-start(bf16[1,2048,704]{1,2,0:T(8,128)(2,1)} %param.16) | copy-start | bytes 8650756
  3.8 13.7 %all-to-all-start = ((bf16[8,16,1]{1,2,0:T(2,128)(2,1)}), bf16[8,16,1]{1,2,0:T(2,128)(2,1)S(1)}, u32[]{:S(2)}, u32[]{:S(2)}) async-start(bf16[8,16,1]{1,2,0:T(2,128)(2,1)} %copy.31), calls=%async_computation | async-start | bytes 8192 | tf_op jit(solution)/shard_map/all_to_all | solution.py:61
  17.5 19.8 %all-to-all-start.2 = ((bf16[8,16,2048]{2,1,0:T(8,128)(2,1)}), bf16[8,16,2048]{2,1,0:T(8,128)(2,1)S(1)}, u32[]{:S(2)}, u32[]{:S(2)}) async-start(bf16[8,16,2048]{2,1,0:T(8,128)(2,1)} %get-tuple-element.16), calls=%async_computation.2 | async-start | bytes 1048576 | tf_op jit(solution)/shard_map/all_to_all | solution.py:59
  37.2 0.8 copy-start.2
  38.0 17.9 %all-to-all-start.1 = ((bf16[8,16,2048]{2,1,0:T(8,128)(2,1)}), bf16[8,16,2048]{2,1,0:T(8,128)(2,1)S(1)}, u32[]{:S(2)}, u32[]{:S(2)}) async-start(bf16[8,16,2048]{2,1,0:T(8,128)(2,1)} %get-tuple-element.17), calls=%async_computation.1 | async-start | bytes 1048576 | tf_op jit(solution)/shard_map/all_to_all | solution.py:60
  58.8 17.5 %copy-start.3 = (bf16[128,704]{0,1:T(8,128)(2,1)S(1)}, bf16[128,704]{0,1:T(8,128)(2,1)}, u32[]{:S(2)}) copy-start(bf16[128,704]{0,1:T(8,128)(2,1)} %get-tuple-element.18) | copy-start | bytes 540676
  59.5 24.8 %copy-start.1 = (bf16[1,2048,704]{1,2,0:T(8,128)(2,1)S(1)}, bf16[1,2048,704]{1,2,0:T(8,128)(2,1)}, u32[]{:S(2)}) copy-start(bf16[1,2048,704]{1,2,0:T(8,128)(2,1)} %param.17) | copy-start | bytes 8650756
  69.0 31.7 %collective-permute-start = (bf16[16,2048]{1,0:T(8,128)(2,1)}, bf16[16,2048]{1,0:T(8,128)(2,1)}, u32[]{:S(2)}, u32[]{:S(2)}) collective-permute-start(bf16[16,2048]{1,0:T(8,128)(2,1)} %get-tuple-element.12), channel_id=1, source_target_pairs={{0,1},{1,0},{2,3},{3,2},{4,5},{5,4},{6,7},{7,6},{8,9},{9,8},{10,11... | collective-permute-start | bytes 196616 | tf_op jit(solution)/shard_map/ppermute | solution.py:25
  70.5 35.5 %collective-permute-start.1 = (bf16[16,2048]{1,0:T(8,128)(2,1)}, bf16[16,2048]{1,0:T(8,128)(2,1)}, u32[]{:S(2)}, u32[]{:S(2)}) collective-permute-start(bf16[16,2048]{1,0:T(8,128)(2,1)} %get-tuple-element.11), channel_id=1, source_target_pairs={{0,2},{1,3},{2,0},{3,1},{4,6},{5,7},{6,4},{7,5},{8,10},{9,11},{10,... | collective-permute-start | bytes 196616 | tf_op jit(solution)/shard_map/ppermute | solution.py:25
  70.5 38.5 %collective-permute-start.2 = (bf16[16,2048]{1,0:T(8,128)(2,1)}, bf16[16,2048]{1,0:T(8,128)(2,1)}, u32[]{:S(2)}, u32[]{:S(2)}) collective-permute-start(bf16[16,2048]{1,0:T(8,128)(2,1)} %get-tuple-element.10), channel_id=1, source_target_pairs={{0,3},{1,2},{2,1},{3,0},{4,7},{5,6},{6,5},{7,4},{8,11},{9,10},{10,... | collective-permute-start | bytes 196616 | tf_op jit(solution)/shard_map/ppermute | solution.py:25
  72.5 37.9 %collective-permute-start.3 = (bf16[16,2048]{1,0:T(8,128)(2,1)}, bf16[16,2048]{1,0:T(8,128)(2,1)}, u32[]{:S(2)}, u32[]{:S(2)}) collective-permute-start(bf16[16,2048]{1,0:T(8,128)(2,1)} %get-tuple-element.9), channel_id=1, source_target_pairs={{0,4},{1,5},{2,6},{3,7},{4,0},{5,1},{6,2},{7,3},{8,12},{9,13},{10,... | collective-permute-start | bytes 196616 | tf_op jit(solution)/shard_map/ppermute | solution.py:25
  72.9 39.0 %collective-permute-start.4 = (bf16[16,2048]{1,0:T(8,128)(2,1)}, bf16[16,2048]{1,0:T(8,128)(2,1)}, u32[]{:S(2)}, u32[]{:S(2)}) collective-permute-start(bf16[16,2048]{1,0:T(8,128)(2,1)} %get-tuple-element.8), channel_id=1, source_target_pairs={{0,5},{1,4},{2,7},{3,6},{4,1},{5,0},{6,3},{7,2},{8,13},{9,12},{10,... | collective-permute-start | bytes 196616 | tf_op jit(solution)/shard_map/ppermute | solution.py:25
  85.6 9.7 %all-to-all-start.3 = ((bf16[8,16,1]{1,2,0:T(2,128)(2,1)}), bf16[8,16,1]{1,2,0:T(2,128)(2,1)S(1)}, u32[]{:S(2)}, u32[]{:S(2)}) async-start(bf16[8,16,1]{1,2,0:T(2,128)(2,1)} %convert_element_type.98), calls=%async_computation.3 | async-start | bytes 8192 | tf_op jit(solution)/shard_map/all_to_all | solution.py:82
  95.3 23.3 %all-to-all-start.4 = ((bf16[128,4,512]{2,0,1:T(8,128)(2,1)}), bf16[128,4,512]{2,0,1:T(8,128)(2,1)}, u32[]{:S(2)}, u32[]{:S(2)}) async-start(bf16[128,4,512]{2,0,1:T(8,128)(2,1)} %copy.34), calls=%async_computation.4 | async-start | bytes 1048576 | tf_op jit(solution)/shard_map/all_to_all | solution.py:85
  100.7 12.6 %collective-permute-start.5 = (bf16[16,2048]{1,0:T(8,128)(2,1)S(1)}, bf16[16,2048]{1,0:T(8,128)(2,1)S(1)}, u32[]{:S(2)}, u32[]{:S(2)}) collective-permute-start(bf16[16,2048]{1,0:T(8,128)(2,1)S(1)} %get-tuple-element.7), channel_id=1, source_target_pairs={{0,6},{1,7},{2,4},{3,5},{4,2},{5,3},{6,0},{7,1},{8,14},{9,15},{10,... | collective-permute-start | bytes 196616 | tf_op jit(solution)/shard_map/ppermute | solution.py:25
  106.0 8.0 %collective-permute-start.6 = (bf16[16,2048]{1,0:T(8,128)(2,1)S(1)}, bf16[16,2048]{1,0:T(8,128)(2,1)S(1)}, u32[]{:S(2)}, u32[]{:S(2)}) collective-permute-start(bf16[16,2048]{1,0:T(8,128)(2,1)S(1)} %get-tuple-element.6), channel_id=1, source_target_pairs={{0,7},{1,6},{2,5},{3,4},{4,3},{5,2},{6,1},{7,0},{8,15},{9,14},{10,... | collective-permute-start | bytes 196616 | tf_op jit(solution)/shard_map/ppermute | solution.py:25
  118.7 13.1 %all-to-all-start.5 = ((bf16[128,4,512]{2,0,1:T(8,128)(2,1)}), bf16[128,4,512]{2,0,1:T(8,128)(2,1)}, u32[]{:S(2)}, u32[]{:S(2)}) async-start(bf16[128,4,512]{2,0,1:T(8,128)(2,1)} %fusion.23), calls=%async_computation.5 | async-start | bytes 1048576 | tf_op jit(solution)/shard_map/all_to_all | solution.py:86
